TPU v7x, 32 devices: a whole 2x2x4 slice. The times are simulated.
32 devices in a mesh: obs: 4 (over z), td: 8 (over y, x, core).
Axes of the slice: x: 2, y: 2, z: 4, core: 2. Of those that a mesh axis runs over, the one named last changes fastest.
Arguments:
- timestreams: bfloat16 [4, 128, 8192], P('obs', 'td'), may hold values from -6 to 6
- filter_taps: bfloat16 [4, 128, 8, 129], P('obs', 'td'), may hold values from -0.5 to 0.5
- scan_bounds: int32 [4, 32], P('obs'), may hold values from 0 to 8192, as said below
- tile_index: int32 [4, 64], P('obs', 'td'), may hold values from 0 to 15
- det_weights: bfloat16 [4, 128], P('obs'), may hold values from 0.29882812 to 3
- positions: float32 [2, 128], replicated, may hold values from -1 to 1
- wafer_group: int32 [128], replicated, may hold values from 0 to 7, as said below
Outputs:
- filtered_residual: float32 [4, 128, 8192], P('obs', 'td')
- sky_map: float32 [16, 128, 128], P(None, ('obs', 'td'))
Inputs may be any that keep to these rules, and one draw needn't show every extreme that they name: `scan_bounds`: each row is strictly increasing, starts with 0 and ends with 8192. `wafer_group`: every wafer group holds the same number of detectors.
All inputs are finite; a program needn't handle non-finite values.
Results may differ from a plain program's by a relative error of at most 0.009.
Values may be sent and summed in bfloat16 or wider, within the bound.
A program may use at most 128 MiB of HBM per device.

v0:
```python
import functools

import jax
import jax.numpy as jnp
from jax import lax
from jax.experimental import pallas as pl
from jax.experimental.pallas import tpu as pltpu
from jax.sharding import PartitionSpec as P

TAPS = 129
HALF = 64
BANDS = 8
TILE = 128
POLY = 6
TILES = 16
LANES = 128
prior_weight = 1.0
F32 = jnp.float32
BF16 = jnp.bfloat16


def lane_band(det):
    return lax.broadcasted_iota(jnp.int32, (HALF, LANES), 1) // det


def projector(pos_ref, wafer_ref, dets):
    x = pos_ref[0:1, :]
    y = pos_ref[1:2, :]
    rows = [jnp.ones_like(x), x, y, x * x, x * y, y * y]
    q = [r.astype(BF16).astype(F32) for r in rows]
    group = jnp.broadcast_to(wafer_ref[...].astype(F32), (dets, dets))
    same = group == group.T
    same_b = jnp.where(same, 1.0, 0.0).astype(BF16)
    pairs = [(i, j) for i in range(POLY) for j in range(i + 1)]
    products = jnp.concatenate(
        [q[i] * q[j] for i, j in pairs] + [jnp.zeros((32 - len(pairs), dets), F32)], axis=0
    )
    high = products.astype(BF16)
    low = (products - high.astype(F32)).astype(BF16)
    gram = jnp.dot(high, same_b, preferred_element_type=F32) + jnp.dot(
        low, same_b, preferred_element_type=F32
    )
    entry = {pair: gram[n : n + 1, :] for n, pair in enumerate(pairs)}
    factor, inv, white = {}, {}, []
    for i in range(POLY):
        for j in range(i + 1):
            value = entry[(i, j)]
            for k in range(j):
                value = value - factor[(i, k)] * factor[(j, k)]
            if i == j:
                factor[(i, i)] = jnp.sqrt(value)
                inv[i] = 1.0 / factor[(i, i)]
            else:
                factor[(i, j)] = value * inv[j]
        value = q[i]
        for k in range(i):
            value = value - factor[(i, k)] * white[k]
        white.append(value * inv[i])
    whitened = jnp.concatenate(white + [jnp.zeros((8 - POLY, dets), F32)], axis=0)
    columns = jnp.concatenate([whitened, jnp.zeros((LANES - 8, dets), F32)], axis=0).T
    outer = columns[:, 0:1] * white[0]
    for m in range(1, POLY):
        outer = outer + columns[:, m : m + 1] * white[m]
    outer = jnp.where(same, outer, 0.0)
    p_high = outer.astype(BF16)
    p_low = (outer - p_high.astype(F32)).astype(BF16)
    return p_high, p_low


def clean(p_high, p_low, gathered):
    fitted = jnp.dot(p_high, gathered, preferred_element_type=F32) + jnp.dot(
        p_low, gathered, preferred_element_type=F32
    )
    return (gathered.astype(F32) - fitted).astype(BF16)


def scan_mask(bounds_ref, length, n_bounds):
    sample = lax.broadcasted_iota(jnp.int32, (BANDS, length), 0) * length + lax.broadcasted_iota(
        jnp.int32, (BANDS, length), 1
    )
    count = jnp.zeros((BANDS, length), jnp.int32)
    for n in range(n_bounds):
        count = count + jnp.where(bounds_ref[0, n] <= sample, 1, 0)
    return (count & 1).astype(F32)


def spread_rows(mask, det):
    return jnp.broadcast_to(mask[:, None, :], (BANDS, det, TILE)).reshape(BANDS * det, TILE)


def own_weights(weights_ref, start, det, dets):
    pick = lax.broadcasted_iota(jnp.int32, (dets, LANES), 0) == start + lax.broadcasted_iota(
        jnp.int32, (dets, LANES), 1
    ) % det
    rows = jnp.broadcast_to(weights_ref[...].astype(F32), (16, dets)).astype(BF16)
    return jnp.dot(rows, jnp.where(pick, 1.0, 0.0).astype(BF16), preferred_element_type=F32)[0:1, :]


def pick_matrix(tiles_row, det):
    shape = (det * TILES, LANES)
    row = lax.broadcasted_iota(jnp.int32, shape, 0)
    lane = lax.broadcasted_iota(jnp.int32, shape, 1)
    hit = (row // TILES == lane % det) & ((row % TILES).astype(F32) == tiles_row)
    return hit


def adjoint_body(pad_ref, taps_ref, ext_ref, out_ref, length, det):
    def chunk(c, _):
        base = pl.multiple_of(c * TILE, TILE)
        acc = jnp.zeros((TILE, LANES), F32)
        for k in range(TAPS):
            acc = acc + taps_ref[k : k + 1, :] * pad_ref[pl.ds(base + (TILE - k), TILE), :]
        ext_ref[pl.ds(base, TILE), :] = acc
        return 0

    lax.fori_loop(0, length // TILE + 1, chunk, 0)
    band = lane_band(det)
    head = ext_ref[0:HALF, :]
    tail = ext_ref[HALF + length : 2 * HALF + length, :]
    ext_ref[length : length + HALF, :] += jnp.where(
        band < BANDS - 1, pltpu.roll(head, LANES - det, 1), 0.0
    )
    ext_ref[HALF : 2 * HALF, :] += jnp.where(band > 0, pltpu.roll(tail, det, 1), 0.0)
    for c in range(length // TILE):
        piece = ext_ref[HALF + c * TILE : HALF + (c + 1) * TILE, :].T
        for b in range(BANDS):
            out_ref[:, b * length + c * TILE : b * length + (c + 1) * TILE] = piece[
                b * det : (b + 1) * det, :
            ]


MESH = pl.DeviceIdType.MESH
PIECES = 4


def load_signal(x_ref, ext_ref, length, det):
    for c in range(length // TILE):
        piece = jnp.concatenate(
            [x_ref[:, b * length + c * TILE : b * length + (c + 1) * TILE] for b in range(BANDS)],
            axis=0,
        )
        ext_ref[HALF + c * TILE : HALF + (c + 1) * TILE, :] = piece.astype(F32).T
    band = lane_band(det)
    last = ext_ref[length : length + HALF, :]
    first = ext_ref[HALF : 2 * HALF, :]
    ext_ref[0:HALF, :] = jnp.where(band > 0, pltpu.roll(last, det, 1), 0.0)
    ext_ref[HALF + length : 2 * HALF + length, :] = jnp.where(
        band < BANDS - 1, pltpu.roll(first, LANES - det, 1), 0.0
    )


def whole_kernel(
    dims, bounds_ref, index_ref, x_ref, taps_ref, weights_ref, pos_ref, wafer_ref,
    out_ref, skyout_ref,
    ext_ref, pad_ref, mask_ref, tiles_ref, fsend, frecv, csend, crecv, tsend, trecv,
    msend, mrecv, nsend, nrecv, sky_ref, skyrecv,
    f_s, f_r, c_s, c_r, t_s, t_r, m_s, m_r, n_s, n_r, k_s, k_r,
):
    n_obs, td, det, length, slab, n_bounds = dims
    dets = det * td
    split = td // BANDS
    blocks = slab // TILE
    width = slab // PIECES
    folds = dets // TILE
    per_fold = td // folds
    parts = n_obs * folds
    own_rows = TILE // (n_obs * td)
    obs = lax.axis_index("obs")
    me = lax.axis_index("td")
    member = obs * folds + me // per_fold

    def td_peer(k):
        return lax.rem(me + k, td)

    def td_source(k):
        return lax.rem(me + td - k, td)

    def part_peer(k):
        m = lax.rem(member + k, parts)
        return (m // folds, lax.rem(me, per_fold) + lax.rem(m, folds) * per_fold)

    def part_source(k):
        return lax.rem(member + parts - k, parts)

    linear = obs * td + me
    target = (lax.rem(me, per_fold) * det) // own_rows + member
    origin_row = linear * own_rows
    origin_member = lax.rem(origin_row, det) // own_rows
    origin = (
        origin_member // folds,
        origin_row // det + lax.rem(origin_member, folds) * per_fold,
    )
    moves = target != linear

    barrier = pltpu.get_barrier_semaphore()
    for k in range(1, td):
        pl.semaphore_signal(barrier, 1, device_id=(obs, td_peer(k)), device_id_type=MESH)
    for k in range(1, parts):
        pl.semaphore_signal(barrier, 1, device_id=part_peer(k), device_id_type=MESH)

    there = (target // td, lax.rem(target, td))
    pl.semaphore_signal(barrier, 1, device_id=there, device_id_type=MESH)
    pl.semaphore_signal(barrier, 1, device_id=origin, device_id_type=MESH)

    row = lax.broadcasted_iota(jnp.int32, (blocks, LANES), 0)
    tile = jnp.zeros((blocks, LANES), jnp.int32)
    for n in range(blocks):
        tile = jnp.where(row == n, index_ref[0, n], tile)
    tsend[...] = tile.astype(F32)
    trecv[me] = tile.astype(F32)
    load_signal(x_ref, ext_ref, length, det)

    def tile_copy(k, slot):
        return pltpu.make_async_remote_copy(
            src_ref=tsend, dst_ref=trecv.at[slot], send_sem=t_s.at[k], recv_sem=t_r.at[k],
            device_id=(obs, td_peer(k)), device_id_type=MESH,
        )

    def signal_copy(h, k, slot):
        cols = pl.ds(pl.multiple_of(h * width, TILE), width)
        peer = td_peer(k)
        return pltpu.make_async_remote_copy(
            src_ref=fsend.at[peer, :, cols], dst_ref=frecv.at[slot, :, cols],
            send_sem=f_s.at[h, k], recv_sem=f_r.at[h, k],
            device_id=(obs, peer), device_id_type=MESH,
        )

    def clean_copy(h, k, slot):
        cols = pl.ds(pl.multiple_of(h * width, TILE), width)
        peer = td_peer(k)
        return pltpu.make_async_remote_copy(
            src_ref=csend.at[peer, :, cols], dst_ref=crecv.at[slot, :, cols],
            send_sem=c_s.at[h, k], recv_sem=c_r.at[h, k],
            device_id=(obs, peer), device_id_type=MESH,
        )

    def hit_copy(k, slot):
        return pltpu.make_async_remote_copy(
            src_ref=msend, dst_ref=mrecv.at[slot], send_sem=m_s.at[k], recv_sem=m_r.at[k],
            device_id=part_peer(k), device_id_type=MESH,
        )

    def sum_copy(k, slot):
        return pltpu.make_async_remote_copy(
            src_ref=nsend, dst_ref=nrecv.at[slot], send_sem=n_s.at[k], recv_sem=n_r.at[k],
            device_id=part_peer(k), device_id_type=MESH,
        )

    def each(count, do):
        def step(k, _):
            do(k)
            return 0

        lax.fori_loop(1, count, step, 0)

    def compute(p):
        quarter = p // PIECES
        h = lax.rem(p, PIECES)

        def chunk(c, _):
            inside = pl.multiple_of(h * width + c * TILE, TILE)
            base = pl.multiple_of(quarter * slab + inside, TILE)
            acc = jnp.zeros((TILE, LANES), F32)
            for k in range(TAPS):
                acc = acc + taps_ref[k : k + 1, :] * ext_ref[pl.ds(base + k, TILE), :]
            block = acc.T.astype(BF16)
            for b in range(BANDS):
                fsend[b * split + quarter, :, pl.ds(inside, TILE)] = block[b * det : (b + 1) * det, :]
            return 0

        lax.fori_loop(0, width // TILE, chunk, 0)

    def send_piece(p):
        quarter = p // PIECES
        h = lax.rem(p, PIECES)

        def send(k):
            if split == 1:
                signal_copy(h, k, me).start()
            else:

                @pl.when(lax.rem(td_peer(k), split) == quarter)
                def _():
                    signal_copy(h, k, me).start()

        each(td, send)

    compute(jnp.int32(0))
    pl.semaphore_wait(barrier, td - 1 + parts - 1 + 2)
    each(td, lambda k: tile_copy(k, me).start())
    send_piece(jnp.int32(0))

    def later(p, _):
        compute(p)
        send_piece(p)
        return 0

    lax.fori_loop(1, split * PIECES, later, 0)
    frecv[me] = fsend[me]

    mask_ref[...] = scan_mask(bounds_ref, length, n_bounds)
    weight_lanes = own_weights(weights_ref, me * det, det, dets)
    each(td, lambda k: tile_copy(k, td_source(k)).wait_recv())
    lane = lax.broadcasted_iota(jnp.int32, (blocks, LANES), 1) // det
    for quarter in range(split):
        tile = trecv[quarter]
        for b in range(1, BANDS):
            tile = jnp.where(lane == b, trecv[b * split + quarter], tile)
        tiles_ref[quarter * blocks : (quarter + 1) * blocks, :] = tile
    first = lax.broadcasted_iota(jnp.int32, (TILES, LANES), 1) % det == 0
    which = lax.broadcasted_iota(jnp.int32, (TILES, LANES), 0).astype(F32)
    counts = jnp.zeros((TILES, TILE), F32)
    for n in range(length // TILE):
        mask = spread_rows(mask_ref[:, n * TILE : (n + 1) * TILE], det).astype(BF16)
        pick = jnp.where(first & (which == tiles_ref[n : n + 1, :]), 1.0, 0.0).astype(BF16)
        counts = counts + jnp.dot(pick, mask, preferred_element_type=F32)
    weight_rows = jnp.broadcast_to(weight_lanes, (LANES, LANES)).T[0:det, :]
    hits = jnp.concatenate([counts, weight_rows], axis=0).astype(BF16)
    msend[...] = hits
    mrecv[member] = hits
    each(parts, lambda k: hit_copy(k, member).start())
    p_high, p_low = projector(pos_ref, wafer_ref, dets)

    for h in range(PIECES):
        each(td, lambda k: signal_copy(h, k, td_source(k)).wait_recv())
        cols = slice(h * width, (h + 1) * width)
        cleaned = clean(p_high, p_low, frecv[:, :, cols].reshape(dets, width))
        csend[:, :, cols] = cleaned.reshape(td, det, width)
        each(td, lambda k: clean_copy(h, k, me).start())
    crecv[me] = csend[me]

    def band_rows(n):
        quarter, inside = n // blocks, n % blocks
        cols = slice(inside * TILE, (inside + 1) * TILE)
        return jnp.concatenate([crecv[b * split + quarter, :, cols] for b in range(BANDS)], axis=0)

    sums = jnp.zeros((det * TILES, TILE), F32)
    for h in range(PIECES):
        each(td, lambda k: clean_copy(h, k, td_source(k)).wait_recv())
        for n in range(length // TILE):
            if (n % blocks) * TILE // width != h:
                continue
            mask = spread_rows(mask_ref[:, n * TILE : (n + 1) * TILE], det)
            masked = (band_rows(n).astype(F32) * mask).astype(BF16)
            pick = jnp.where(pick_matrix(tiles_ref[n : n + 1, :], det), weight_lanes, 0.0)
            sums = sums + jnp.dot(pick.astype(BF16), masked, preferred_element_type=F32)
    nsend[...] = sums.astype(BF16)
    nrecv[member] = sums.astype(BF16)
    each(parts, lambda k: sum_copy(k, member).start())
    each(parts, lambda k: hit_copy(k, part_source(k)).wait_recv())
    hit = jnp.zeros((det, TILES, TILE), F32)
    for m in range(parts):
        part = mrecv[m].astype(F32)
        hit = hit + part[TILES:, None, :] * part[None, :TILES, :]
    each(parts, lambda k: sum_copy(k, part_source(k)).wait_recv())
    total = nrecv[0].astype(F32)
    for m in range(1, parts):
        total = total + nrecv[m].astype(F32)
    sky = total / (hit.reshape(det * TILES, TILE) + prior_weight)
    sky_ref[...] = sky
    give = pl.ds(pl.multiple_of(member * own_rows * TILES, TILES), own_rows * TILES)
    row_copy = pltpu.make_async_remote_copy(
        src_ref=sky_ref.at[give], dst_ref=skyrecv, send_sem=k_s, recv_sem=k_r,
        device_id=(target // td, lax.rem(target, td)), device_id_type=MESH,
    )

    @pl.when(moves)
    def _():
        row_copy.start()

    @pl.when(jnp.logical_not(moves))
    def _():
        skyrecv[...] = sky_ref[give, :]

    sky_b = sky.astype(BF16)
    zero = jnp.zeros((TILE, LANES), F32)
    pad_ref[0:TILE, :] = zero
    pad_ref[TILE + length : 2 * TILE + length, :] = zero
    for n in range(length // TILE):
        mask = spread_rows(mask_ref[:, n * TILE : (n + 1) * TILE], det)
        pick = jnp.where(pick_matrix(tiles_ref[n : n + 1, :], det), 1.0, 0.0)
        chosen = jnp.dot(pick.T.astype(BF16), sky_b, preferred_element_type=F32)
        residual = (mask * (band_rows(n).astype(F32) - chosen)).astype(BF16)
        pad_ref[TILE + n * TILE : 2 * TILE + n * TILE, :] = residual.astype(F32).T
    adjoint_body(pad_ref, taps_ref, ext_ref, out_ref, length, det)

    @pl.when(moves)
    def _():
        row_copy.wait()

    for d in range(own_rows):
        skyout_ref[:, d, :] = skyrecv[d * TILES : (d + 1) * TILES, :]
    each(td, lambda k: tile_copy(k, me).wait_send())
    for h in range(PIECES):
        each(td, lambda k: signal_copy(h, k, me).wait_send())
        each(td, lambda k: clean_copy(h, k, me).wait_send())
    each(parts, lambda k: hit_copy(k, member).wait_send())
    each(parts, lambda k: sum_copy(k, member).wait_send())


VM = pl.BlockSpec(memory_space=pltpu.VMEM)
SM = pl.BlockSpec(memory_space=pltpu.SMEM)


def local(timestreams, filter_taps, scan_bounds, tile_index, det_weights, positions, wafer_group):
    _, det, samples = timestreams.shape
    td = lax.axis_size("td")
    n_obs = lax.axis_size("obs")
    dets = det * td
    length = samples // BANDS
    slab = samples // td
    blocks = slab // TILE
    parts = n_obs * (dets // TILE)
    own_rows = TILE // (n_obs * td)
    dims = (n_obs, td, det, length, slab, scan_bounds.shape[1])
    taps = jnp.transpose(filter_taps[0], (2, 1, 0)).reshape(TAPS, BANDS * det).astype(F32)
    dma = pltpu.SemaphoreType.DMA
    out, sky = pl.pallas_call(
        functools.partial(whole_kernel, dims),
        out_shape=(
            jax.ShapeDtypeStruct((det, samples), F32),
            jax.ShapeDtypeStruct((TILES, own_rows, TILE), F32),
        ),
        in_specs=[SM, SM, VM, VM, VM, VM, VM],
        out_specs=(VM, VM),
        scratch_shapes=[
            pltpu.VMEM((length + 2 * HALF, LANES), F32),
            pltpu.VMEM((length + 2 * TILE, LANES), F32),
            pltpu.VMEM((BANDS, length), F32),
            pltpu.VMEM((length // TILE, LANES), F32),
            pltpu.VMEM((td, det, slab), BF16),
            pltpu.VMEM((td, det, slab), BF16),
            pltpu.VMEM((td, det, slab), BF16),
            pltpu.VMEM((td, det, slab), BF16),
            pltpu.VMEM((blocks, LANES), F32),
            pltpu.VMEM((td, blocks, LANES), F32),
            pltpu.VMEM((TILES + det, TILE), BF16),
            pltpu.VMEM((parts, TILES + det, TILE), BF16),
            pltpu.VMEM((det * TILES, TILE), BF16),
            pltpu.VMEM((parts, det * TILES, TILE), BF16),
            pltpu.VMEM((det * TILES, TILE), F32),
            pltpu.VMEM((own_rows * TILES, TILE), F32),
            dma((PIECES, td)), dma((PIECES, td)), dma((PIECES, td)), dma((PIECES, td)),
            dma((td,)), dma((td,)), dma((parts,)), dma((parts,)),
            dma((parts,)), dma((parts,)),
            dma, dma,
        ],
        compiler_params=pltpu.CompilerParams(
            collective_id=0, has_side_effects=True, vmem_limit_bytes=48 << 20
        ),
    )(
        scan_bounds, tile_index, timestreams[0], taps, det_weights, positions,
        wafer_group.reshape(1, dets),
    )
    return out[None], sky


def solution(mesh):
    placed = (
        P("obs", "td", None),
        P("obs", "td", None, None),
        P("obs", None),
        P("obs", "td"),
        P("obs", None),
        P(),
        P(),
    )
    return jax.shard_map(
        local,
        mesh=mesh,
        in_specs=placed,
        out_specs=(P("obs", "td", None), P(None, ("obs", "td"), None)),
        check_vma=False,
    )
```

profile of v0, /device:TPU:0, one launch (start us, length us, event | category | flops | bytes accessed | tf_op | source)
XLA Modules:
  0.0 37.7 jit_solution(3218143879223408616)
XLA Ops:
  0.6 0.9 %convert_bitcast_fusion = f32[129,8,16]{0,1,2:T(8,128)S(1)} fusion(bf16[1,16,8,129]{3,2,1,0:T(8,128)(2,1)} %param.8), kind=kLoop, calls=%fused_computation | loop fusion | flops 16512 | bytes 99072 | tf_op jit(solution)/shard_map/convert_element_type | solution.py:416
  1.5 0.0 copy-start
  1.5 0.0 copy-start.1
  1.6 0.0 copy-start.2
  1.6 0.0 copy-start.3
  1.6 0.0 copy-start.4
  1.6 0.0 copy-start.5
  1.6 0.1 copy.11.taps_ref
  1.7 0.7 %copy-done = bf16[1,16,8192]{2,1,0:T(8,128)(2,1)S(1)} copy-done((bf16[1,16,8192]{2,1,0:T(8,128)(2,1)S(1)}, bf16[1,16,8192]{2,1,0:T(8,128)(2,1)}, u32[]{:S(2)}) %copy-start) | copy-done | bytes 262168
  2.4 0.0 copy-done.1
  2.4 0.0 copy-done.2
  2.4 0.0 copy-done.3
  2.4 0.0 copy-done.4
  2.4 0.0 copy-done.5
  2.5 33.8 %shard_map.86 = (f32[16,8192]{1,0:T(8,128)S(1)}, f32[16,4,128]{2,1,0:T(4,128)S(1)}) custom-call(s32[1,32]{1,0:T(1,128)S(1)} %copy-done.2, s32[1,8]{1,0:T(1,128)S(1)} %copy-done.3, bf16[16,8192]{1,0:T(8,128)(2,1)S(1)} %bitcast.10, f32[129,128]{1,0:T(8,128)S(1)} %copy.11.taps_ref, bf16[1,128]{1,0:T(2,128)(2,1)S(1)} %copy-done.4, f32[2,128]{1,0:T(2,128)S(1)} %copy-done.1, ...), custom_call_target="tpu_custom_call" | custom-call | tf_op jit(solution)/shard_map/pallas_call | solution.py:418
  36.3 0.8 %copy.14 = f32[1,16,8192]{2,1,0:T(8,128)} copy(f32[1,16,8192]{2,1,0:T(8,128)S(1)} %bitcast.9) | data formatting | bytes 1048576
  37.1 0.6 %copy.15 = f32[16,4,128]{2,1,0:T(4,128)} copy(f32[16,4,128]{2,1,0:T(4,128)S(1)} %get-tuple-element.9) | data formatting | bytes 65536
  (1 shorter events, 0.0 us)
Async XLA Ops:
  1.5 1.0 %copy-start = (bf16[1,16,8192]{2,1,0:T(8,128)(2,1)S(1)}, bf16[1,16,8192]{2,1,0:T(8,128)(2,1)}, u32[]{:S(2)}) copy-start(bf16[1,16,8192]{2,1,0:T(8,128)(2,1)} %param.7) | copy-start | bytes 786436
  1.5 0.9 %copy-start.1 = (f32[2,128]{1,0:T(2,128)S(1)}, f32[2,128]{1,0:T(2,128)}, u32[]{:S(2)}) copy-start(f32[2,128]{1,0:T(2,128)} %pos_ref.1) | copy-start | bytes 3076
  1.6 0.9 %copy-start.2 = (s32[1,32]{1,0:T(1,128)S(1)}, s32[1,32]{1,0:T(1,128)}, u32[]{:S(2)}) copy-start(s32[1,32]{1,0:T(1,128)} %bounds_ref.1) | copy-start | bytes 388
  1.6 0.9 %copy-start.3 = (s32[1,8]{1,0:T(1,128)S(1)}, s32[1,8]{1,0:T(1,128)}, u32[]{:S(2)}) copy-start(s32[1,8]{1,0:T(1,128)} %index_ref.1) | copy-start | bytes 100
  1.6 0.9 %copy-start.4 = (bf16[1,128]{1,0:T(2,128)(2,1)S(1)}, bf16[1,128]{1,0:T(2,128)(2,1)}, u32[]{:S(2)}) copy-start(bf16[1,128]{1,0:T(2,128)(2,1)} %weights_ref.1) | copy-start | bytes 772
  1.6 0.9 %copy-start.5 = (s32[128]{0:T(128)S(1)}, s32[128]{0:T(128)}, u32[]{:S(2)}) copy-start(s32[128]{0:T(128)} %param.13) | copy-start | bytes 1540
where the time goes:
time: 37.9 us; the launch traced here: 37.7 us
  Pallas kernels  33.8 us (89%)
  local copies, waits for them, and re-layouts  2.31 us (6%)
  other arithmetic  0.85 us (2%)
  between operations  0.72 us (2%)
    pallas_call x1, Pallas kernels, local(): pl.pallas_call(functools.partial(whole_kernel, dims), out_shape=(jax.Shap...  33.8 us
    unnamed x14, local copies, waits for them, and re-layouts  2.18 us
    convert_element_type x1, other arithmetic, local(): jnp.transpose(filter_taps[0], (2, 1, 0)).reshape(TAPS, BANDS * det)  0.85 us

commit v1 on v0

--- a/solution.py
+++ b/solution.py
@@ -74,18 +74,14 @@
     return (gathered.astype(F32) - fitted).astype(BF16)
 
 
-def scan_mask(bounds_ref, length, n_bounds):
-    sample = lax.broadcasted_iota(jnp.int32, (BANDS, length), 0) * length + lax.broadcasted_iota(
-        jnp.int32, (BANDS, length), 1
-    )
-    count = jnp.zeros((BANDS, length), jnp.int32)
+def scan_mask(bounds_ref, rows, n_bounds):
+    sample = lax.broadcasted_iota(jnp.int32, (rows, TILE), 0) * TILE + lax.broadcasted_iota(
+        jnp.int32, (rows, TILE), 1
+    )
+    count = jnp.zeros((rows, TILE), jnp.int32)
     for n in range(n_bounds):
         count = count + jnp.where(bounds_ref[0, n] <= sample, 1, 0)
     return (count & 1).astype(F32)
-
-
-def spread_rows(mask, det):
-    return jnp.broadcast_to(mask[:, None, :], (BANDS, det, TILE)).reshape(BANDS * det, TILE)
 
 
 def own_weights(weights_ref, start, det, dets):
@@ -96,37 +92,38 @@
     return jnp.dot(rows, jnp.where(pick, 1.0, 0.0).astype(BF16), preferred_element_type=F32)[0:1, :]
 
 
-def pick_matrix(tiles_row, det):
-    shape = (det * TILES, LANES)
-    row = lax.broadcasted_iota(jnp.int32, shape, 0)
-    lane = lax.broadcasted_iota(jnp.int32, shape, 1)
-    hit = (row // TILES == lane % det) & ((row % TILES).astype(F32) == tiles_row)
-    return hit
-
-
-def adjoint_body(pad_ref, taps_ref, ext_ref, out_ref, length, det):
-    def chunk(c, _):
-        base = pl.multiple_of(c * TILE, TILE)
-        acc = jnp.zeros((TILE, LANES), F32)
-        for k in range(TAPS):
-            acc = acc + taps_ref[k : k + 1, :] * pad_ref[pl.ds(base + (TILE - k), TILE), :]
-        ext_ref[pl.ds(base, TILE), :] = acc
+def load_taps(raw_ref, low_ref, last_ref, taps_ref, det):
+    for d in range(det):
+        value = raw_ref[d].astype(F32)
+        low_ref[d * BANDS : (d + 1) * BANDS, :] = value[:, 0:LANES]
+        last_ref[d * BANDS : (d + 1) * BANDS, :] = jnp.broadcast_to(
+            value[:, LANES:TAPS], (BANDS, LANES)
+        )
+    low = [low_ref[pl.ds(b, det, stride=BANDS), :] for b in range(BANDS)]
+    last = [last_ref[pl.ds(b, det, stride=BANDS), :] for b in range(BANDS)]
+    taps_ref[0:LANES, :] = jnp.concatenate(low, axis=0).T
+    taps_ref[LANES:TAPS, :] = jnp.concatenate(last, axis=0).T[0:1, :]
+
+
+def build_toeplitz(low_ref, last_ref, toep_ref, det):
+    lead = lax.broadcasted_iota(jnp.int32, (TILE, LANES), 1) - lax.broadcasted_iota(
+        jnp.int32, (TILE, LANES), 0
+    )
+    inner = (lead >= -HALF) & (lead < HALF)
+
+    def one(d, _):
+        for b in range(BANDS):
+            n = d * BANDS + b
+            row = jnp.broadcast_to(low_ref[pl.ds(n, 1), :], (TILE, LANES))
+            last = jnp.broadcast_to(last_ref[pl.ds(n, 1), :], (TILE, LANES))
+            ring = pltpu.roll(row, HALF, 1, stride=1, stride_axis=0)
+            here = jnp.where(inner, ring, jnp.where(lead == HALF, last, 0.0))
+            away = jnp.where(inner, jnp.where(lead == -HALF, last, 0.0), ring)
+            toep_ref[n, :, 0:LANES] = here.astype(BF16)
+            toep_ref[n, :, LANES : 2 * LANES] = away.astype(BF16)
         return 0
 
-    lax.fori_loop(0, length // TILE + 1, chunk, 0)
-    band = lane_band(det)
-    head = ext_ref[0:HALF, :]
-    tail = ext_ref[HALF + length : 2 * HALF + length, :]
-    ext_ref[length : length + HALF, :] += jnp.where(
-        band < BANDS - 1, pltpu.roll(head, LANES - det, 1), 0.0
-    )
-    ext_ref[HALF : 2 * HALF, :] += jnp.where(band > 0, pltpu.roll(tail, det, 1), 0.0)
-    for c in range(length // TILE):
-        piece = ext_ref[HALF + c * TILE : HALF + (c + 1) * TILE, :].T
-        for b in range(BANDS):
-            out_ref[:, b * length + c * TILE : b * length + (c + 1) * TILE] = piece[
-                b * det : (b + 1) * det, :
-            ]
+    lax.fori_loop(0, det, one, 0)
 
 
 MESH = pl.DeviceIdType.MESH
@@ -150,11 +147,12 @@
 
 
 def whole_kernel(
-    dims, bounds_ref, index_ref, x_ref, taps_ref, weights_ref, pos_ref, wafer_ref,
+    dims, bounds_ref, index_ref, x_hbm, taps_hbm, weights_ref, pos_ref, wafer_ref,
     out_ref, skyout_ref,
-    ext_ref, pad_ref, mask_ref, tiles_ref, fsend, frecv, csend, crecv, tsend, trecv,
+    x_ref, raw_ref, low_ref, last_ref, taps_ref, toep_ref, clean_ref, edge_ref, wide_ref,
+    ext_ref, mask_ref, fsend, frecv, csend, crecv, tsend, trecv,
     msend, mrecv, nsend, nrecv, sky_ref, skyrecv,
-    f_s, f_r, c_s, c_r, t_s, t_r, m_s, m_r, n_s, n_r, k_s, k_r,
+    f_s, f_r, c_s, c_r, t_s, t_r, m_s, m_r, n_s, n_r, k_s, k_r, in_s,
 ):
     n_obs, td, det, length, slab, n_bounds = dims
     dets = det * td
@@ -182,25 +180,19 @@
     def part_source(k):
         return lax.rem(member + parts - k, parts)
 
-    linear = obs * td + me
-    target = (lax.rem(me, per_fold) * det) // own_rows + member
-    origin_row = linear * own_rows
-    origin_member = lax.rem(origin_row, det) // own_rows
-    origin = (
-        origin_member // folds,
-        origin_row // det + lax.rem(origin_member, folds) * per_fold,
-    )
-    moves = target != linear
+    fold = me // per_fold
+    first_row = own_rows * (obs * td + fold * per_fold)
+    row_source = fold * per_fold + (own_rows * (obs * td + me)) // det
+    x_copy = pltpu.make_async_copy(x_hbm, x_ref, in_s.at[0])
+    raw_copy = pltpu.make_async_copy(taps_hbm, raw_ref, in_s.at[1])
+    x_copy.start()
+    raw_copy.start()
 
     barrier = pltpu.get_barrier_semaphore()
     for k in range(1, td):
         pl.semaphore_signal(barrier, 1, device_id=(obs, td_peer(k)), device_id_type=MESH)
     for k in range(1, parts):
         pl.semaphore_signal(barrier, 1, device_id=part_peer(k), device_id_type=MESH)
-
-    there = (target // td, lax.rem(target, td))
-    pl.semaphore_signal(barrier, 1, device_id=there, device_id_type=MESH)
-    pl.semaphore_signal(barrier, 1, device_id=origin, device_id_type=MESH)
 
     row = lax.broadcasted_iota(jnp.int32, (blocks, LANES), 0)
     tile = jnp.zeros((blocks, LANES), jnp.int32)
@@ -208,6 +200,9 @@
         tile = jnp.where(row == n, index_ref[0, n], tile)
     tsend[...] = tile.astype(F32)
     trecv[me] = tile.astype(F32)
+    raw_copy.wait()
+    load_taps(raw_ref, low_ref, last_ref, taps_ref, det)
+    x_copy.wait()
     load_signal(x_ref, ext_ref, length, det)
 
     def tile_copy(k, slot):
@@ -286,7 +281,7 @@
         each(td, send)
 
     compute(jnp.int32(0))
-    pl.semaphore_wait(barrier, td - 1 + parts - 1 + 2)
+    pl.semaphore_wait(barrier, td - 1 + parts - 1)
     each(td, lambda k: tile_copy(k, me).start())
     send_piece(jnp.int32(0))
 
@@ -298,22 +293,15 @@
     lax.fori_loop(1, split * PIECES, later, 0)
     frecv[me] = fsend[me]
 
-    mask_ref[...] = scan_mask(bounds_ref, length, n_bounds)
+    rows = length * BANDS // TILE
+    mask_ref[...] = scan_mask(bounds_ref, rows, n_bounds)
     weight_lanes = own_weights(weights_ref, me * det, det, dets)
     each(td, lambda k: tile_copy(k, td_source(k)).wait_recv())
-    lane = lax.broadcasted_iota(jnp.int32, (blocks, LANES), 1) // det
-    for quarter in range(split):
-        tile = trecv[quarter]
-        for b in range(1, BANDS):
-            tile = jnp.where(lane == b, trecv[b * split + quarter], tile)
-        tiles_ref[quarter * blocks : (quarter + 1) * blocks, :] = tile
-    first = lax.broadcasted_iota(jnp.int32, (TILES, LANES), 1) % det == 0
-    which = lax.broadcasted_iota(jnp.int32, (TILES, LANES), 0).astype(F32)
-    counts = jnp.zeros((TILES, TILE), F32)
-    for n in range(length // TILE):
-        mask = spread_rows(mask_ref[:, n * TILE : (n + 1) * TILE], det).astype(BF16)
-        pick = jnp.where(first & (which == tiles_ref[n : n + 1, :]), 1.0, 0.0).astype(BF16)
-        counts = counts + jnp.dot(pick, mask, preferred_element_type=F32)
+    which = lax.broadcasted_iota(jnp.int32, (rows, LANES), 1).astype(F32)
+    chosen_tile = jnp.where(trecv[...].reshape(rows, LANES) == which, 1.0, 0.0)
+    by_block = chosen_tile[:, 0:TILES].astype(BF16)
+    by_tile = chosen_tile.T[0:TILES, :].astype(BF16)
+    counts = jnp.dot(by_tile, mask_ref[...].astype(BF16), preferred_element_type=F32)
     weight_rows = jnp.broadcast_to(weight_lanes, (LANES, LANES)).T[0:det, :]
     hits = jnp.concatenate([counts, weight_rows], axis=0).astype(BF16)
     msend[...] = hits
@@ -329,24 +317,21 @@
         each(td, lambda k: clean_copy(h, k, me).start())
     crecv[me] = csend[me]
 
-    def band_rows(n):
-        quarter, inside = n // blocks, n % blocks
-        cols = slice(inside * TILE, (inside + 1) * TILE)
-        return jnp.concatenate([crecv[b * split + quarter, :, cols] for b in range(BANDS)], axis=0)
-
-    sums = jnp.zeros((det * TILES, TILE), F32)
     for h in range(PIECES):
         each(td, lambda k: clean_copy(h, k, td_source(k)).wait_recv())
-        for n in range(length // TILE):
+        for n in range(rows):
             if (n % blocks) * TILE // width != h:
                 continue
-            mask = spread_rows(mask_ref[:, n * TILE : (n + 1) * TILE], det)
-            masked = (band_rows(n).astype(F32) * mask).astype(BF16)
-            pick = jnp.where(pick_matrix(tiles_ref[n : n + 1, :], det), weight_lanes, 0.0)
-            sums = sums + jnp.dot(pick.astype(BF16), masked, preferred_element_type=F32)
-    nsend[...] = sums.astype(BF16)
-    nrecv[member] = sums.astype(BF16)
+            inside = n % blocks
+            cols = slice(inside * TILE, (inside + 1) * TILE)
+            clean_ref[n * det : (n + 1) * det, :] = crecv[n // blocks, :, cols].astype(F32)
+    for d in range(det):
+        masked = (clean_ref[pl.ds(d, rows, stride=det), :] * mask_ref[...]).astype(BF16)
+        sums = jnp.dot(by_tile, masked, preferred_element_type=F32) * weight_rows[d : d + 1, :]
+        nsend[d * TILES : (d + 1) * TILES, :] = sums.astype(BF16)
+    nrecv[member] = nsend[...]
     each(parts, lambda k: sum_copy(k, member).start())
+    build_toeplitz(low_ref, last_ref, toep_ref, det)
     each(parts, lambda k: hit_copy(k, part_source(k)).wait_recv())
     hit = jnp.zeros((det, TILES, TILE), F32)
     for m in range(parts):
@@ -358,36 +343,58 @@
         total = total + nrecv[m].astype(F32)
     sky = total / (hit.reshape(det * TILES, TILE) + prior_weight)
     sky_ref[...] = sky
-    give = pl.ds(pl.multiple_of(member * own_rows * TILES, TILES), own_rows * TILES)
-    row_copy = pltpu.make_async_remote_copy(
-        src_ref=sky_ref.at[give], dst_ref=skyrecv, send_sem=k_s, recv_sem=k_r,
-        device_id=(target // td, lax.rem(target, td)), device_id_type=MESH,
-    )
-
-    @pl.when(moves)
+    def row_place(j):
+        return pl.ds(pl.multiple_of(lax.rem(first_row + own_rows * j, det) * TILES, TILES), own_rows * TILES)
+
+    def row_copy(j):
+        return pltpu.make_async_remote_copy(
+            src_ref=sky_ref.at[row_place(j)], dst_ref=skyrecv, send_sem=k_s.at[j], recv_sem=k_r,
+            device_id=(obs, fold * per_fold + j), device_id_type=MESH,
+        )
+
+    def row_moves(do):
+        for j in range(per_fold):
+            holds = (first_row + own_rows * j) // det == lax.rem(me, per_fold)
+
+            @pl.when(holds & (fold * per_fold + j != me))
+            def _():
+                do(j)
+
+    row_moves(lambda j: row_copy(j).start())
+
+    @pl.when(row_source == me)
     def _():
-        row_copy.start()
-
-    @pl.when(jnp.logical_not(moves))
+        skyrecv[...] = sky_ref[row_place(lax.rem(me, per_fold)), :]
+
+    sky_b = sky.astype(BF16)
+    zero = jnp.zeros((8, LANES), F32)
+    near = lax.broadcasted_iota(jnp.int32, (rows, LANES), 1) < HALF
+    per_band = rows // BANDS
+    for d in range(det):
+        picked = jnp.dot(by_block, sky_b[d * TILES : (d + 1) * TILES, :], preferred_element_type=F32)
+        residual = mask_ref[...] * (clean_ref[pl.ds(d, rows, stride=det), :] - picked)
+        spread = [
+            jnp.dot(
+                residual[b * per_band : (b + 1) * per_band, :].astype(BF16),
+                toep_ref[d * BANDS + b],
+                preferred_element_type=F32,
+            )
+            for b in range(BANDS)
+        ]
+        edge_ref[d, 0:8, :] = zero
+        edge_ref[d, 8 + rows : 16 + rows, :] = zero
+        edge_ref[d, 8 : 8 + rows, :] = jnp.concatenate([p[:, LANES:] for p in spread], axis=0)
+        here = jnp.concatenate([p[:, :LANES] for p in spread], axis=0)
+        away = jnp.where(near, edge_ref[d, 7 : 7 + rows, :], edge_ref[d, 9 : 9 + rows, :])
+        wide_ref[pl.ds(d, rows, stride=det), :] = here + away
+    for n in range(rows):
+        out_ref[:, n * TILE : (n + 1) * TILE] = wide_ref[n * det : (n + 1) * det, :]
+
+    @pl.when(row_source != me)
     def _():
-        skyrecv[...] = sky_ref[give, :]
-
-    sky_b = sky.astype(BF16)
-    zero = jnp.zeros((TILE, LANES), F32)
-    pad_ref[0:TILE, :] = zero
-    pad_ref[TILE + length : 2 * TILE + length, :] = zero
-    for n in range(length // TILE):
-        mask = spread_rows(mask_ref[:, n * TILE : (n + 1) * TILE], det)
-        pick = jnp.where(pick_matrix(tiles_ref[n : n + 1, :], det), 1.0, 0.0)
-        chosen = jnp.dot(pick.T.astype(BF16), sky_b, preferred_element_type=F32)
-        residual = (mask * (band_rows(n).astype(F32) - chosen)).astype(BF16)
-        pad_ref[TILE + n * TILE : 2 * TILE + n * TILE, :] = residual.astype(F32).T
-    adjoint_body(pad_ref, taps_ref, ext_ref, out_ref, length, det)
-
-    @pl.when(moves)
-    def _():
-        row_copy.wait()
-
+        row_copy(0).wait_recv()
+
+    row_moves(lambda j: row_copy(j).wait_send())
     for d in range(own_rows):
         skyout_ref[:, d, :] = skyrecv[d * TILES : (d + 1) * TILES, :]
     each(td, lambda k: tile_copy(k, me).wait_send())
@@ -400,6 +407,7 @@
 
 VM = pl.BlockSpec(memory_space=pltpu.VMEM)
 SM = pl.BlockSpec(memory_space=pltpu.SMEM)
+HB = pl.BlockSpec(memory_space=pltpu.HBM)
 
 
 def local(timestreams, filter_taps, scan_bounds, tile_index, det_weights, positions, wafer_group):
@@ -413,7 +421,7 @@
     parts = n_obs * (dets // TILE)
     own_rows = TILE // (n_obs * td)
     dims = (n_obs, td, det, length, slab, scan_bounds.shape[1])
-    taps = jnp.transpose(filter_taps[0], (2, 1, 0)).reshape(TAPS, BANDS * det).astype(F32)
+    rows = samples // TILE
     dma = pltpu.SemaphoreType.DMA
     out, sky = pl.pallas_call(
         functools.partial(whole_kernel, dims),
@@ -421,13 +429,20 @@
             jax.ShapeDtypeStruct((det, samples), F32),
             jax.ShapeDtypeStruct((TILES, own_rows, TILE), F32),
         ),
-        in_specs=[SM, SM, VM, VM, VM, VM, VM],
+        in_specs=[SM, SM, HB, HB, VM, VM, VM],
         out_specs=(VM, VM),
         scratch_shapes=[
+            pltpu.VMEM((det, samples), BF16),
+            pltpu.VMEM((det, BANDS, TAPS), BF16),
+            pltpu.VMEM((det * BANDS, LANES), F32),
+            pltpu.VMEM((det * BANDS, LANES), F32),
+            pltpu.VMEM((TAPS, LANES), F32),
+            pltpu.VMEM((det * BANDS, TILE, 2 * LANES), BF16),
+            pltpu.VMEM((rows * det, TILE), F32),
+            pltpu.VMEM((det, rows + 16, LANES), F32),
+            pltpu.VMEM((rows * det, TILE), F32),
             pltpu.VMEM((length + 2 * HALF, LANES), F32),
-            pltpu.VMEM((length + 2 * TILE, LANES), F32),
-            pltpu.VMEM((BANDS, length), F32),
-            pltpu.VMEM((length // TILE, LANES), F32),
+            pltpu.VMEM((rows, TILE), F32),
             pltpu.VMEM((td, det, slab), BF16),
             pltpu.VMEM((td, det, slab), BF16),
             pltpu.VMEM((td, det, slab), BF16),
@@ -443,13 +458,13 @@
             dma((PIECES, td)), dma((PIECES, td)), dma((PIECES, td)), dma((PIECES, td)),
             dma((td,)), dma((td,)), dma((parts,)), dma((parts,)),
             dma((parts,)), dma((parts,)),
-            dma, dma,
+            dma((td // (dets // TILE),)), dma, dma((2,)),
         ],
         compiler_params=pltpu.CompilerParams(
             collective_id=0, has_side_effects=True, vmem_limit_bytes=48 << 20
         ),
     )(
-        scan_bounds, tile_index, timestreams[0], taps, det_weights, positions,
+        scan_bounds, tile_index, timestreams[0], filter_taps[0], det_weights, positions,
         wafer_group.reshape(1, dets),
     )
     return out[None], sky

time: 37.9 us -> 33.7 us (0.89)
  Pallas kernels: 33.8 us -> 28.9 us
  local copies, waits for them, and re-layouts: 2.31 us -> 3.89 us
  other arithmetic: 0.85 us -> 0 us
    pallas_call x1, Pallas kernels: 33.8 us -> 28.9 us  [local(): pl.pallas_call(functools.partial(whole_kernel, dims), out_shape=(jax.Shap...]
    unnamed x14 -> x16, local copies, waits for them, and re-layouts: 2.18 us -> 3.89 us
    convert_element_type x1 -> x0, other arithmetic: 0.85 us -> none  [local(): jnp.transpose(filter_taps[0], (2, 1, 0)).reshape(TAPS, BANDS * det)]
where the time goes in v1:
time: 33.7 us; the launch traced here: 33.5 us
  Pallas kernels  28.9 us (86%)
  local copies, waits for them, and re-layouts  3.89 us (12%)
  between operations  0.68 us (2%)
    pallas_call x1, Pallas kernels, local(): pl.pallas_call(functools.partial(whole_kernel, dims), out_shape=(jax.Shap...  28.9 us
    unnamed x16, local copies, waits for them, and re-layouts  3.89 us

profile of v1, /device:TPU:0, one launch (start us, length us, event | category | flops | bytes accessed | tf_op | source)
XLA Modules:
  0.0 33.5 jit_solution(2461739592568563308)
XLA Ops:
  0.6 0.0 copy-start.4
  0.6 0.0 copy-start.5
  0.7 0.0 copy-start.6
  0.7 0.0 copy-start.2
  0.7 0.0 copy-start.3
  0.7 0.6 %copy-done.4 = s32[1,8]{1,0:T(1,128)S(1)} copy-done((s32[1,8]{1,0:T(1,128)S(1)}, s32[1,8]{1,0:T(1,128)}, u32[]{:S(2)}) %copy-start.4) | copy-done | bytes 56
  1.3 0.0 copy-done.5
  1.3 0.0 copy-done.6
  1.3 0.0 copy-done.2
  1.4 0.0 copy-done.3
  1.4 0.0 copy-start
  1.4 0.9 %copy-done = bf16[1,16,8192]{2,1,0:T(8,128)(2,1)S(1)} copy-done((bf16[1,16,8192]{2,1,0:T(8,128)(2,1)S(1)}, bf16[1,16,8192]{2,1,0:T(8,128)(2,1)}, u32[]{:S(2)}) %copy-start) | copy-done | bytes 262168
  2.3 0.0 copy-start.1
  2.3 0.8 %copy-done.1 = bf16[1,16,8,129]{3,2,1,0:T(8,128)(2,1)S(1)} copy-done((bf16[1,16,8,129]{3,2,1,0:T(8,128)(2,1)S(1)}, bf16[1,16,8,129]{3,2,1,0:T(8,128)(2,1)}, u32[]{:S(2)}) %copy-start.1) | copy-done | bytes 33048
  3.2 28.9 %shard_map.86 = (f32[16,8192]{1,0:T(8,128)S(1)}, f32[16,4,128]{2,1,0:T(4,128)S(1)}) custom-call(s32[1,32]{1,0:T(1,128)S(1)} %copy-done.3, s32[1,8]{1,0:T(1,128)S(1)} %copy-done.4, bf16[16,8192]{1,0:T(8,128)(2,1)S(1)} %bitcast.5, bf16[16,8,129]{2,1,0:T(8,128)(2,1)S(1)} %bitcast.6, bf16[1,128]{1,0:T(2,128)(2,1)S(1)} %copy-done.5, f32[2,128]{1,0:T(2,128)S(1)} %copy-done.2, ...), custom_call_target="tpu_custom_call" | custom-call | tf_op jit(solution)/shard_map/pallas_call | solution.py:426
  32.1 0.8 %copy.11 = f32[1,16,8192]{2,1,0:T(8,128)} copy(f32[1,16,8192]{2,1,0:T(8,128)S(1)} %bitcast.4) | data formatting | bytes 1048576
  32.9 0.6 %copy.12 = f32[16,4,128]{2,1,0:T(4,128)} copy(f32[16,4,128]{2,1,0:T(4,128)S(1)} %get-tuple-element.9) | data formatting | bytes 65536
Async XLA Ops:
  0.6 0.7 %copy-start.4 = (s32[1,8]{1,0:T(1,128)S(1)}, s32[1,8]{1,0:T(1,128)}, u32[]{:S(2)}) copy-start(s32[1,8]{1,0:T(1,128)} %index_ref.1) | copy-start | bytes 100
  0.6 0.7 %copy-start.5 = (bf16[1,128]{1,0:T(2,128)(2,1)S(1)}, bf16[1,128]{1,0:T(2,128)(2,1)}, u32[]{:S(2)}) copy-start(bf16[1,128]{1,0:T(2,128)(2,1)} %weights_ref.1) | copy-start | bytes 772
  0.7 0.7 %copy-start.6 = (s32[128]{0:T(128)S(1)}, s32[128]{0:T(128)}, u32[]{:S(2)}) copy-start(s32[128]{0:T(128)} %param.13) | copy-start | bytes 1540
  0.7 0.7 %copy-start.2 = (f32[2,128]{1,0:T(2,128)S(1)}, f32[2,128]{1,0:T(2,128)}, u32[]{:S(2)}) copy-start(f32[2,128]{1,0:T(2,128)} %pos_ref.1) | copy-start | bytes 3076
  0.7 0.7 %copy-start.3 = (s32[1,32]{1,0:T(1,128)S(1)}, s32[1,32]{1,0:T(1,128)}, u32[]{:S(2)}) copy-start(s32[1,32]{1,0:T(1,128)} %bounds_ref.1) | copy-start | bytes 388
  1.4 1.0 %copy-start = (bf16[1,16,8192]{2,1,0:T(8,128)(2,1)S(1)}, bf16[1,16,8192]{2,1,0:T(8,128)(2,1)}, u32[]{:S(2)}) copy-start(bf16[1,16,8192]{2,1,0:T(8,128)(2,1)} %param.7) | copy-start | bytes 786436
  2.3 0.8 %copy-start.1 = (bf16[1,16,8,129]{3,2,1,0:T(8,128)(2,1)S(1)}, bf16[1,16,8,129]{3,2,1,0:T(8,128)(2,1)}, u32[]{:S(2)}) copy-start(bf16[1,16,8,129]{3,2,1,0:T(8,128)(2,1)} %param.8) | copy-start | bytes 99076
